TPU v7x, 256 devices: a whole 4x4x8 slice. The times are simulated.
256 devices in a mesh: br: 8 (over y_lo, x), bus: 32 (over y_hi, z, core).
Axes of the slice: x: 4, y: 4 (y_hi: 2, y_lo: 2; y = y_hi * 2 + y_lo), z: 8, core: 2. Of those that a mesh axis runs over, the one named last changes fastest.
Arguments:
- ptdf: bfloat16 [8192, 65536], P('br', 'bus'), may hold values from -0.0234375 to 0.0234375
- load_codes: int32 [65536, 1024], P('bus'), may hold values from -4096 to 4096
- limit_codes: int32 [8192], P('br'), may hold values from 64 to 320
Outputs:
- penalty: float32 [8192, 1024], P(('br', 'bus'))
- sensitivity: float32 [65536, 1024], P('bus', 'br')
All inputs are finite; a program needn't handle non-finite values.
Results may differ from a plain program's by a relative error of at most 0.004.
Values may be sent and summed in bfloat16 or wider, within the bound.
A program may use at most 128 MiB of HBM per device.

v0:
```python
import jax
import jax.numpy as jnp
from jax import lax
from jax.sharding import PartitionSpec as P


def overload(flows, limit_codes):
    limits = (limit_codes.astype(jnp.float32) / 64.0)[:, None]
    magnitude = jnp.sqrt(flows * flows + 1.0)
    zvalue = 4.0 * (magnitude / limits - 1.0)
    penalty = jax.nn.softplus(zvalue) / 4.0
    adjoint = (jax.nn.sigmoid(zvalue) * flows / (magnitude * limits)).astype(jnp.bfloat16)
    return (penalty, adjoint)


def local(ptdf, load_codes, limit_codes):
    injections = (load_codes.astype(jnp.float32) / 1024.0).astype(jnp.bfloat16)
    branch_local = ptdf.shape[0]
    owned = branch_local // lax.axis_size("bus")
    offset = lax.axis_index("bus") * owned
    partial_flows = jnp.dot(ptdf, injections, preferred_element_type=jnp.float32)
    flows = lax.psum_scatter(partial_flows, "bus", scatter_dimension=0, tiled=True)
    limits_own = lax.dynamic_slice_in_dim(limit_codes, offset, owned, 0)
    penalty, adjoint_own = overload(flows, limits_own)
    adjoint_block = lax.all_gather(adjoint_own, "bus", axis=0, tiled=True)
    partial_sens = lax.dot_general(
        ptdf, adjoint_block, (((0,), (0,)), ((), ())), preferred_element_type=jnp.float32
    )
    sensitivity = lax.psum_scatter(partial_sens, "br", scatter_dimension=1, tiled=True)
    return (penalty, sensitivity)


def solution(mesh):
    return jax.shard_map(
        local,
        mesh=mesh,
        in_specs=(P("br", "bus"), P("bus", None), P("br")),
        out_specs=(P(("br", "bus"), None), P("bus", "br")),
        check_vma=False,
    )
```

profile of v0, /device:TPU:1, one launch (start us, length us, event | category | flops | bytes accessed | tf_op | source)
XLA Modules:
  0.0 348.7 jit_solution(4985150040851442825)
XLA Ops:
  7.2 0.0 reduce-scatter.7.cloned.1.call-start
  7.2 11.1 %fusion.2 = f32[1024,1024]{0,1:T(8,128)} fusion(bf16[1024,2048]{1,0:T(8,128)(2,1)} %param.3, s32[2048,1024]{1,0:T(8,128)} %param.4), kind=kOutput, calls=%fused_computation.4 | convolution fusion | flops 4301258752 | bytes 16777216 | tf_op jit(solution)/shard_map/dot_general | solution.py:21
  18.3 5.3 %copy.14 = f32[1024,1024]{1,0:T(8,128)} copy(f32[1024,1024]{0,1:T(8,128)} %fusion.2) | data formatting | bytes 8388608
  23.6 0.0 reduce-scatter.7.cloned.1.call-update
  23.7 0.0 all-gather.2.cloned.1.call-start
  23.7 0.8 convert_multiply_fusion
  24.5 126.7 %reduce-scatter.7.cloned.1.call-done = f32[32,1024]{1,0:T(8,128)} async-done(((f32[1024,1024]{1,0:T(8,128)}), f32[32,1024]{1,0:T(8,128)}) %reduce-scatter.7.cloned.1.call-update) | async-done | bytes 131088 | tf_op jit(solution)/shard_map/reduce_scatter | solution.py:22
  151.1 1.8 divide_convert_fusion
  152.9 0.0 all-gather.2.cloned.1.call-update
  153.0 0.0 reduce-scatter.5.cloned.1.call-start
  153.0 84.4 %all-gather.2.cloned.1.call-done = bf16[1024,1024]{1,0:T(8,128)(2,1)} async-done(((bf16[32,1024]{1,0:T(8,128)(2,1)}), bf16[1024,1024]{1,0:T(8,128)(2,1)}) %all-gather.2.cloned.1.call-update) | async-done | bytes 2097168 | tf_op jit(solution)/shard_map/all_gather | solution.py:25
  237.4 10.6 %convolution_bitcast_fusion = f32[2048,1024]{0,1:T(8,128)} fusion(bf16[1024,1024]{1,0:T(8,128)(2,1)} %all-gather.2.cloned.1.call-done, bf16[1024,2048]{1,0:T(8,128)(2,1)} %param.3), kind=kOutput, calls=%fused_computation.1 | convolution fusion | flops 4294967296 | bytes 14680064 | tf_op jit(solution)/shard_map/dot_general | solution.py:26
  248.0 0.0 reduce-scatter.5.cloned.1.call-update
  248.0 91.6 %reduce-scatter.5.cloned.1.call-done = f32[2048,128]{0,1:T(8,128)} async-done(((f32[2048,1024]{0,1:T(8,128)}), f32[2048,128]{0,1:T(8,128)}) %reduce-scatter.5.cloned.1.call-update) | async-done | bytes 1048592 | tf_op jit(solution)/shard_map/reduce_scatter | solution.py:29
  339.6 2.5 copy.13
Async XLA Ops:
  7.2 144.0 %reduce-scatter.7.cloned.1.call-start = ((), (), s32[]{:S(2)}) async-start(), calls=%async_computation.4 | async-start | bytes 4325376 | tf_op jit(solution)/shard_map/reduce_scatter | solution.py:22
  23.7 213.7 %all-gather.2.cloned.1.call-start = ((), (), s32[]{:S(2)}) async-start(), calls=%async_computation.2 | async-start | bytes 2162688 | tf_op jit(solution)/shard_map/all_gather | solution.py:25
  153.0 186.7 %reduce-scatter.5.cloned.1.call-start = ((), (), s32[]{:S(2)}) async-start(), calls=%async_computation.3 | async-start | bytes 9437184 | tf_op jit(solution)/shard_map/reduce_scatter | solution.py:29
Sparse Core Ops, SparseCore 0:
  23.8 127.3 reduce-scatter.6
  154.9 82.4 all-gather.1
  248.2 91.4 reduce-scatter.4
where the time goes:
time: 349 us
  waiting for transfers between devices  303 us (87%)
  matrix products  21.7 us (6%)
  between operations  13.7 us (4%)
  local copies, waits for them, and re-layouts  7.88 us (2%)
    reduce_scatter x1, waiting for transfers between devices, local(): lax.psum_scatter(partial_flows, 'bus', scatter_dimension=0, tiled=True)  127 us
    reduce_scatter x1, waiting for transfers between devices, local(): lax.psum_scatter(partial_sens, 'br', scatter_dimension=1, tiled=True)  91.6 us
    all_gather x1, waiting for transfers between devices, local(): adjoint_block = lax.all_gather(adjoint_own, 'bus', axis=0, tiled=True)  84.4 us
    dot_general x1, matrix products, local(): jnp.dot(ptdf, injections, preferred_element_type=jnp.float32)  11.1 us
    dot_general x1, matrix products, local(): lax.dot_general(ptdf, adjoint_block, (((0,), (0,)), ((), ())), preferred_...  10.6 us
    unnamed x2, local copies, waits for them, and re-layouts  7.88 us
  transfers between devices with their start and end apart: 3, of which 3 were waited for; matrix products, arithmetic and copies ran while one was open for 0% of the time, Pallas kernels for 0%

commit v1 on v0

--- a/solution.py
+++ b/solution.py
@@ -22,7 +22,9 @@
     flows = lax.psum_scatter(partial_flows, "bus", scatter_dimension=0, tiled=True)
     limits_own = lax.dynamic_slice_in_dim(limit_codes, offset, owned, 0)
     penalty, adjoint_own = overload(flows, limits_own)
-    adjoint_block = lax.all_gather(adjoint_own, "bus", axis=0, tiled=True)
+    adjoint_block = jnp.concatenate(
+        lax.all_to_all(jnp.stack([adjoint_own] * lax.axis_size("bus")), "bus", 0, 0), axis=0
+    )
     partial_sens = lax.dot_general(
         ptdf, adjoint_block, (((0,), (0,)), ((), ())), preferred_element_type=jnp.float32
     )

time: 349 us -> 324 us (0.928)
  waiting for transfers between devices: 303 us -> 220 us
  blocking collectives: 0 us -> 60.7 us
  matrix products: 21.7 us -> 18 us
    all_gather x1 -> x0, waiting for transfers between devices: 84.4 us -> none  [local(): adjoint_block = lax.all_gather(adjoint_own, 'bus', axis=0, tiled=True)]
    all_to_all x0 -> x1, blocking collectives: none -> 60.7 us  [local(): lax.all_to_all(jnp.stack([adjoint_own] * lax.axis_size('bus')), 'bus', 0, 0)]
    dot_general x1, matrix products: 10.6 us -> 6.87 us  [local(): lax.dot_general(ptdf, adjoint_block, (((0,), (0,)), ((), ())), preferred_...]
    unnamed x2 -> x4, local copies, waits for them, and re-layouts: 7.88 us -> 7.87 us
  transfers between devices with their start and end apart: 3 -> 2, of which waited for: 3 -> 2; matrix products, arithmetic and copies ran while one was open for 0% -> 0% of each run, Pallas kernels for 0% -> 0%
where the time goes in v1:
time: 324 us
  waiting for transfers between devices  220 us (68%)
  blocking collectives  60.7 us (19%)
  matrix products  18 us (6%)
  between operations  14.1 us (4%)
  local copies, waits for them, and re-layouts  8.12 us (3%)
    reduce_scatter x1, waiting for transfers between devices, local(): lax.psum_scatter(partial_flows, 'bus', scatter_dimension=0, tiled=True)  127 us
    reduce_scatter x1, waiting for transfers between devices, local(): lax.psum_scatter(partial_sens, 'br', scatter_dimension=1, tiled=True)  93.4 us
    all_to_all x1, blocking collectives, local(): lax.all_to_all(jnp.stack([adjoint_own] * lax.axis_size('bus')), 'bus', 0, 0)  60.7 us
    dot_general x1, matrix products, local(): jnp.dot(ptdf, injections, preferred_element_type=jnp.float32)  11.1 us
    unnamed x4, local copies, waits for them, and re-layouts  7.87 us
    dot_general x1, matrix products, local(): lax.dot_general(ptdf, adjoint_block, (((0,), (0,)), ((), ())), preferred_...  6.87 us
  transfers between devices with their start and end apart: 2, of which 2 were waited for; matrix products, arithmetic and copies ran while one was open for 0% of the time, Pallas kernels for 0%

profile of v1, /device:TPU:1, one launch (start us, length us, event | category | flops | bytes accessed | tf_op | source)
XLA Modules:
  0.0 323.7 jit_solution(6220440145703991227)
XLA Ops:
  7.2 0.0 reduce-scatter.7.cloned.1.call-start
  7.2 11.1 %fusion.2 = f32[1024,1024]{0,1:T(8,128)} fusion(bf16[1024,2048]{1,0:T(8,128)(2,1)} %param.3, s32[2048,1024]{1,0:T(8,128)} %param.4), kind=kOutput, calls=%fused_computation.4 | convolution fusion | flops 4301258752 | bytes 16777216 | tf_op jit(solution)/shard_map/dot_general | solution.py:21
  18.3 5.3 %copy.15 = f32[1024,1024]{1,0:T(8,128)} copy(f32[1024,1024]{0,1:T(8,128)} %fusion.2) | data formatting | bytes 8388608
  23.6 0.0 reduce-scatter.7.cloned.1.call-update
  23.7 0.0 reduce-scatter.5.cloned.1.call-start
  23.7 0.8 convert_multiply_fusion
  24.5 126.7 %reduce-scatter.7.cloned.1.call-done = f32[32,1024]{1,0:T(8,128)} async-done(((f32[1024,1024]{1,0:T(8,128)}), f32[32,1024]{1,0:T(8,128)}) %reduce-scatter.7.cloned.1.call-update) | async-done | bytes 131088 | tf_op jit(solution)/shard_map/reduce_scatter | solution.py:22
  151.1 0.0 copy-start
  151.1 1.9 divide_convert_fusion
  153.1 0.2 stack.2
  153.3 60.7 %all_to_all.5 = bf16[32,32,1024]{2,1,0:T(8,128)(2,1)S(1)} all-to-all(bf16[32,32,1024]{2,1,0:T(8,128)(2,1)S(1)} %stack.2), channel_id=1, replica_groups=mesh['br'=8,'bus'=32] {'bus'}, dimensions={0} | all-to-all | bytes 4194304 | tf_op jit(solution)/shard_map/all_to_all | solution.py:26
  214.0 0.0 copy-done
  214.0 6.9 %convolution_bitcast_fusion = f32[2048,1024]{0,1:T(8,128)} fusion(bf16[1024,1024]{1,0:T(8,128)(2,1)S(1)} %bitcast.9, bf16[1024,2048]{1,0:T(8,128)(2,1)S(1)} %copy-done), kind=kOutput, calls=%fused_computation.1 | convolution fusion | flops 4294967296 | bytes 14680064 | tf_op jit(solution)/shard_map/dot_general | solution.py:28
  220.9 0.0 reduce-scatter.5.cloned.1.call-update
  220.9 93.4 %reduce-scatter.5.cloned.1.call-done = f32[2048,128]{0,1:T(8,128)} async-done(((f32[2048,1024]{0,1:T(8,128)}), f32[2048,128]{0,1:T(8,128)}) %reduce-scatter.5.cloned.1.call-update) | async-done | bytes 1048592 | tf_op jit(solution)/shard_map/reduce_scatter | solution.py:31
  314.3 2.5 copy.14
Async XLA Ops:
  7.2 144.0 %reduce-scatter.7.cloned.1.call-start = ((), (), s32[]{:S(2)}) async-start(), calls=%async_computation.4 | async-start | bytes 4325376 | tf_op jit(solution)/shard_map/reduce_scatter | solution.py:22
  23.7 290.6 %reduce-scatter.5.cloned.1.call-start = ((), (), s32[]{:S(2)}) async-start(), calls=%async_computation.3 | async-start | bytes 9437184 | tf_op jit(solution)/shard_map/reduce_scatter | solution.py:31
  151.1 62.9 %copy-start = (bf16[1024,2048]{1,0:T(8,128)(2,1)S(1)}, bf16[1024,2048]{1,0:T(8,128)(2,1)}, u32[]{:S(2)}) copy-start(bf16[1024,2048]{1,0:T(8,128)(2,1)} %param.3) | copy-start | bytes 12582916
Sparse Core Ops, SparseCore 0:
  23.8 127.3 reduce-scatter.6
  221.0 93.1 reduce-scatter.4
